TPU v7x, 256 devices: a whole 4x4x8 slice. The times are simulated.
256 devices in a mesh: pair: 32 (over z, y), red: 8 (over x, core).
Axes of the slice: x: 4, y: 4, z: 8, core: 2. Of those that a mesh axis runs over, the one named last changes fastest.
Arguments:
- amplitudes: bfloat16 [2048, 512, 640], P('pair', 'red'), may hold values from -6 to 6
- cycle_integrals: bfloat16 [640, 640], P('pair'), may hold values from -0.5 to 0.5
- ladder_integrals: bfloat16 [32, 8, 1280, 512], P('pair', 'red'), may hold values from -0.125 to 0.125
- orbital_irrep: int32 [640], replicated, may hold values from 0 to 7, as said below
- pair_irrep: int32 [2048], P('pair'), may hold values from 0 to 7, as said below
- tile_owners: int32 [8, 320], replicated, may hold values from 0 to 319, each once within a row
- ladder_tiles: int32 [32, 4], replicated, may hold values from 0 to 2559
Outputs:
- ladder_block: bfloat16 [32, 2048, 512], P('pair', 'red')
Inputs may be any that keep to these rules, and one draw needn't show every extreme that they name: Each row of tile_owners is a permutation of 0 .. 319. `orbital_irrep`: nondecreasing along the virtual orbitals; the first is 0 and the last 7. A program must be right for any labels meeting these rules, including one irrep holding nearly all orbitals. `pair_irrep`: A program must be right for any labels in the range, in any mixture.
All inputs are finite; a program needn't handle non-finite values.
Results may differ from a plain program's by a relative error of at most 0.019.
Values may be sent and summed in bfloat16 or wider, within the bound.
A program may use at most 128 MiB of HBM per device.

v0:
```python
import jax
import jax.numpy as jnp
from jax import lax
from jax.sharding import PartitionSpec as P


def irrep_lookup(irreps, indices):
    table_ids = jnp.arange(irreps.shape[0], dtype=jnp.int32)
    return jnp.sum(jnp.where(indices[..., None] == table_ids, irreps, 0), axis=-1)


def shards(
    amplitudes,
    cycle_integrals,
    ladder_integrals,
    orbital_irrep,
    pair_irrep,
    tile_owners,
    ladder_tiles,
):
    pair_count = lax.axis_size("pair")
    pair_index = lax.axis_index("pair")
    red_index = lax.axis_index("red")
    local_pairs, slab_rows, width_all = amplitudes.shape
    block_count = width_all // 128
    a_local = red_index * slab_rows + jnp.arange(slab_rows, dtype=jnp.int32)
    irrep_slab = irrep_lookup(orbital_irrep, a_local)
    allowed = (
        jnp.bitwise_xor(irrep_slab[:, None], orbital_irrep[None, :])[None]
        == pair_irrep[:, None, None]
    )
    symmetric = jnp.where(allowed, amplitudes, jnp.zeros_like(amplitudes))
    cycle_rows = cycle_integrals.shape[0]
    c_local = pair_index * cycle_rows + jnp.arange(cycle_rows, dtype=jnp.int32)
    cycle_keep = irrep_lookup(orbital_irrep, c_local)[:, None] == orbital_irrep[None, :]
    blocked = jnp.where(cycle_keep, cycle_integrals, jnp.zeros_like(cycle_integrals))
    flattened = symmetric.reshape(local_pairs * slab_rows, width_all)
    gathered_cycle = lax.all_gather(blocked, "pair", axis=0, tiled=True)
    cycle = jnp.dot(flattened, gathered_cycle, preferred_element_type=jnp.float32)
    dressed = (flattened.astype(jnp.float32) + cycle).astype(jnp.bfloat16)
    tiles_local = dressed.reshape(local_pairs, slab_rows * block_count, 128)
    slot_order = lax.dynamic_index_in_dim(tile_owners, red_index, 0, keepdims=False)
    owned_count = slot_order.shape[0] // pair_count
    ordered = jnp.take(tiles_local, slot_order, axis=1).reshape(
        local_pairs, pair_count, owned_count, 128
    )
    lane_ids = jnp.arange(128, dtype=jnp.int32)
    mine_tiles = lax.dynamic_slice_in_dim(slot_order, pair_index * owned_count, owned_count, 0)
    a_rows = red_index * slab_rows + mine_tiles // block_count
    b_cols = (mine_tiles % block_count)[:, None] * 128 + lane_ids
    irrep_cd = jnp.bitwise_xor(
        irrep_lookup(orbital_irrep, a_rows)[:, None], irrep_lookup(orbital_irrep, b_cols)
    ).reshape(-1)
    batch_ids = ladder_tiles[pair_index]
    a_out = batch_ids // block_count
    b_out = (batch_ids % block_count)[:, None] * 128 + lane_ids
    irrep_ab = jnp.bitwise_xor(
        irrep_lookup(orbital_irrep, a_out)[:, None], irrep_lookup(orbital_irrep, b_out)
    ).reshape(-1)
    weights = ladder_integrals[0, 0]
    masked = jnp.where(irrep_cd[:, None] == irrep_ab[None, :], weights, jnp.zeros_like(weights))
    total_rows = local_pairs * pair_count
    received = lax.all_to_all(ordered, "pair", split_axis=1, concat_axis=0, tiled=True)
    owned = received.reshape(total_rows, owned_count * 128)
    result = lax.psum_scatter(
        jnp.dot(owned, masked, preferred_element_type=jnp.float32).astype(jnp.bfloat16),
        "red",
        scatter_dimension=0,
        tiled=True,
    )
    return result[None]


def solution(mesh):
    return jax.shard_map(
        shards,
        mesh=mesh,
        in_specs=(
            P("pair", "red", None),
            P("pair", None),
            P("pair", "red", None, None),
            P(),
            P("pair"),
            P(),
            P(),
        ),
        out_specs=P("pair", "red", None),
        check_vma=False,
    )
```

profile of v0, /device:TPU:8, one launch (start us, length us, event | category | flops | bytes accessed | tf_op | source)
XLA Modules:
  0.0 275.5 jit_solution(3836330692513094179)
XLA Ops:
  6.5 0.7 fusion.14
  7.3 0.7 dynamic-slice_reduce_fusion
  8.0 0.9 select_reduce_fusion.2
  8.9 0.8 broadcast_xor_fusion
  9.7 0.9 select_reduce_fusion.3
  10.5 0.8 fusion.11
  11.4 53.0 %all-gather = bf16[32,20,640]{2,1,0:T(8,128)(2,1)S(1)} all-gather(bf16[1,20,640]{2,1,0:T(8,128)(2,1)S(1)} %fusion.11), channel_id=1, replica_groups=mesh['pair'=32,'red'=8] {'pair'}, dimensions={0}, use_global_device_ids=true | all-gather | bytes 844800 | tf_op jit(solution)/shard_map/all_gather | solution.py:38
  64.6 4.0 %compare_select_fusion = bf16[64,64,640]{2,1,0:T(8,128)(2,1)S(1)} fusion(bf16[64,64,640]{2,1,0:T(8,128)(2,1)} %param.7, s32[64,640]{1,0:T(8,128)S(1)} %broadcast_xor_fusion, s32[64]{0:T(128)} %param.11), kind=kLoop, calls=%fused_computation.2 | loop fusion | flops 5242880 | bytes 10649856 | tf_op jit(solution)/shard_map/jit(_where)/select_n | solution.py:32
  68.6 6.8 %add_convert_fusion = bf16[4096,640]{1,0:T(8,128)(2,1)} fusion(bf16[4096,640]{1,0:T(8,128)(2,1)S(1)} %bitcast.46, bf16[640,640]{1,0:T(8,128)(2,1)S(1)} %reshape.277), kind=kOutput, calls=%fused_computation.1 | convolution fusion | flops 3363307520 | bytes 11304960 | tf_op jit(solution)/shard_map/dot_general | solution.py:39
  75.4 9.4 %reshape.266 = bf16[64,320,128]{2,1,0:T(8,128)(2,1)} reshape(bf16[4096,640]{1,0:T(8,128)(2,1)} %add_convert_fusion) | data formatting | bytes 10485760 | tf_op jit(solution)/shard_map/reshape | solution.py:41
  84.8 8.2 %copy.12 = bf16[64,320,128]{2,0,1:T(8,128)(2,1)} copy(bf16[64,320,128]{2,1,0:T(8,128)(2,1)} %reshape.266) | data formatting | bytes 10485760 | tf_op jit(solution)/shard_map/reshape | solution.py:41
  93.2 6.1 %gather_fusion = bf16[320,64,128]{2,1,0:T(8,128)(2,1)} fusion(bf16[64,320,128]{2,0,1:T(8,128)(2,1)} %copy.12, s32[1024]{0:T(1024)S(1)} %pad_clamp_fusion), kind=kCustom, calls=%fused_computation | custom fusion | bytes 10487040 | tf_op jit(solution)/shard_map/jit(_take)/gather | solution.py:44
  99.3 5.9 %broadcast_select_fusion = bf16[64,32,10,128]{3,0,2,1:T(8,128)(2,1)} fusion(bf16[64,32,10,128]{3,0,2,1:T(8,128)(2,1)} %bitcast.44, pred[32,10]{1,0:T(8,128)(4,1)S(1)} %compare_and_fusion), kind=kLoop, calls=%fused_computation.6 | loop fusion | flops 2621440 | bytes 10486080 | tf_op jit(solution)/shard_map/jit(_take)/select_n | solution.py:44
  105.3 6.8 %all-to-all-start = ((bf16[64,32,10,128]{3,0,2,1:T(8,128)(2,1)}), bf16[64,32,10,128]{3,0,2,1:T(8,128)(2,1)}, u32[]{:S(2)}, u32[]{:S(2)}) async-start(bf16[64,32,10,128]{3,0,2,1:T(8,128)(2,1)} %broadcast_select_fusion), calls=%async_computation | async-start | bytes 10485760 | tf_op jit(solution)/shard_map/all_to_all | solution.py:63
  112.1 0.2 reduce-scatter.2.cloned.1.call-start
  112.3 0.2 fusion.12
  112.5 0.2 divide_reduce_fusion
  112.7 0.8 fusion.17
  114.0 0.3 select_reduce_fusion.1
  114.3 0.6 select_reduce_fusion
  115.1 104.2 %all-to-all-done = bf16[64,32,10,128]{3,0,2,1:T(8,128)(2,1)} async-done(((bf16[64,32,10,128]{3,0,2,1:T(8,128)(2,1)}), bf16[64,32,10,128]{3,0,2,1:T(8,128)(2,1)}, u32[]{:S(2)}, u32[]{:S(2)}) %all-to-all-start) | async-done | bytes 5242912 | tf_op jit(solution)/shard_map/all_to_all | solution.py:63
  219.3 11.8 %copy.13 = bf16[32,64,1,10,128]{4,3,1,0,2:T(8,128)(2,1)S(1)} copy(bf16[32,64,1,10,128]{4,1,3,0,2:T(8,128)(2,1)} %bitcast.6) | data formatting | bytes 10485760 | tf_op jit(solution)/shard_map/all_to_all | solution.py:63
  231.1 4.4 %fusion.3 = bf16[2048,512]{1,0:T(8,128)(2,1)} fusion(bf16[256,8,10,128]{3,2,1,0:T(8,128)(2,1)S(1)} %bitcast.45, bf16[1,1,1280,512]{3,2,1,0:T(8,128)(2,1)S(1)} %copy-done.2, s32[512]{0:T(512)S(1)} %xor_bitcast_fusion.1, s32[1280]{0:T(1024)S(1)} %xor_bitcast_fusion), kind=kOutput, calls=%fused_computation.9 | convolution fusion | flops 2686713856 | bytes 8657920 | tf_op jit(solution)/shard_map/dot_general | solution.py:66
  235.5 33.2 %reduce-scatter.2.cloned.1.call-done = bf16[256,512]{1,0:T(8,128)(2,1)} async-done(((bf16[2048,512]{1,0:T(8,128)(2,1)}), bf16[256,512]{1,0:T(8,128)(2,1)}) %reduce-scatter.2.cloned.1.call-update) | async-done | bytes 262160 | tf_op jit(solution)/shard_map/reduce_scatter | solution.py:65
  (20 shorter events, 1.0 us)
Async XLA Ops:
  105.3 7.0 %copy-start.1 = (s32[32,4]{0,1:T(4,128)S(1)}, s32[32,4]{0,1:T(4,128)}, u32[]{:S(2)}) copy-start(s32[32,4]{0,1:T(4,128)} %param.13) | copy-start | bytes 1540
  105.3 8.2 %copy-start = (s32[640]{0:T(1024)S(1)}, s32[640]{0:T(1024)}, u32[]{:S(2)}) copy-start(s32[640]{0:T(1024)} %param.10) | copy-start | bytes 7684
  105.3 114.0 %all-to-all-start = ((bf16[64,32,10,128]{3,0,2,1:T(8,128)(2,1)}), bf16[64,32,10,128]{3,0,2,1:T(8,128)(2,1)}, u32[]{:S(2)}, u32[]{:S(2)}) async-start(bf16[64,32,10,128]{3,0,2,1:T(8,128)(2,1)} %broadcast_select_fusion), calls=%async_computation | async-start | bytes 10485760 | tf_op jit(solution)/shard_map/all_to_all | solution.py:63
  112.1 156.6 %reduce-scatter.2.cloned.1.call-start = ((), (), s32[]{:S(2)}) async-start(), calls=%async_computation.2 | async-start | bytes 2359296 | tf_op jit(solution)/shard_map/reduce_scatter | solution.py:65
  219.3 11.8 %copy-start.2 = (bf16[1,1,1280,512]{3,2,1,0:T(8,128)(2,1)S(1)}, bf16[1,1,1280,512]{3,2,1,0:T(8,128)(2,1)}, u32[]{:S(2)}) copy-start(bf16[1,1,1280,512]{3,2,1,0:T(8,128)(2,1)} %param.9) | copy-start | bytes 3932164
Sparse Core Ops, SparseCore 0:
  235.6 33.0 reduce-scatter.1
where the time goes:
time: 276 us
  waiting for transfers between devices  137 us (50%)
  blocking collectives  53 us (19%)
  local copies, waits for them, and re-layouts  36.6 us (13%)
  other arithmetic  16.8 us (6%)
  between operations  13.5 us (5%)
  matrix products  11.2 us (4%)
  starting transfers between devices  7.01 us (3%)
    all_to_all x1, waiting for transfers between devices, shards(): lax.all_to_all(ordered, 'pair', split_axis=1, concat_axis=0, tiled=True)  104 us
    all_gather x1, blocking collectives, shards(): gathered_cycle = lax.all_gather(blocked, 'pair', axis=0, tiled=True)  53 us
    reduce_scatter x1, waiting for transfers between devices, shards(): lax.psum_scatter(jnp.dot(owned, masked, preferred_element_type=jnp.float3...  33.2 us
    reshape x2, local copies, waits for them, and re-layouts, shards(): tiles_local = dressed.reshape(local_pairs, slab_rows * block_count, 128)  17.6 us
    all_to_all x1, local copies, waits for them, and re-layouts, shards(): lax.all_to_all(ordered, 'pair', split_axis=1, concat_axis=0, tiled=True)  11.8 us
    dot_general x1, matrix products, shards(): jnp.dot(flattened, gathered_cycle, preferred_element_type=jnp.float32)  6.8 us
    all_to_all x1, starting transfers between devices, shards(): lax.all_to_all(ordered, 'pair', split_axis=1, concat_axis=0, tiled=True)  6.79 us
    select_n x2, other arithmetic, shards(): jnp.take(tiles_local, slot_order, axis=1)  6.67 us
  transfers between devices with their start and end apart: 2, of which 2 were waited for; matrix products, arithmetic and copies ran while one was open for 1% of the time, Pallas kernels for 0%

commit v1 on v0

--- a/solution.py
+++ b/solution.py
@@ -35,7 +35,9 @@
     cycle_keep = irrep_lookup(orbital_irrep, c_local)[:, None] == orbital_irrep[None, :]
     blocked = jnp.where(cycle_keep, cycle_integrals, jnp.zeros_like(cycle_integrals))
     flattened = symmetric.reshape(local_pairs * slab_rows, width_all)
-    gathered_cycle = lax.all_gather(blocked, "pair", axis=0, tiled=True)
+    gathered_cycle = jnp.concatenate(
+        lax.all_to_all(jnp.stack([blocked] * lax.axis_size("pair")), "pair", 0, 0), axis=0
+    )
     cycle = jnp.dot(flattened, gathered_cycle, preferred_element_type=jnp.float32)
     dressed = (flattened.astype(jnp.float32) + cycle).astype(jnp.bfloat16)
     tiles_local = dressed.reshape(local_pairs, slab_rows * block_count, 128)

time: 276 us -> 267 us (0.967)
  blocking collectives: 53 us -> 0 us
  waiting for transfers between devices: 137 us -> 164 us
  starting transfers between devices: 7.01 us -> 17.7 us
  matrix products: 11.2 us -> 14.8 us
    all_gather x1 -> x0, blocking collectives: 53 us -> none  [shards(): gathered_cycle = lax.all_gather(blocked, 'pair', axis=0, tiled=True)]
    all_to_all x0 -> x1, waiting for transfers between devices: none -> 17 us  [shards(): lax.all_to_all(jnp.stack([blocked] * lax.axis_size('pair')), 'pair', 0, 0)]
    all_to_all x0 -> x1, starting transfers between devices: none -> 11.7 us  [shards(): lax.all_to_all(jnp.stack([blocked] * lax.axis_size('pair')), 'pair', 0, 0)]
    all_to_all x1, waiting for transfers between devices: 104 us -> 115 us  [shards(): lax.all_to_all(ordered, 'pair', split_axis=1, concat_axis=0, tiled=True)]
    dot_general x1, matrix products: 6.8 us -> 10.5 us  [shards(): jnp.dot(flattened, gathered_cycle, preferred_element_type=jnp.float32)]
  transfers between devices with their start and end apart: 2 -> 3, of which waited for: 2 -> 3; matrix products, arithmetic and copies ran while one was open for 1% -> 5% of each run, Pallas kernels for 0% -> 0%
where the time goes in v1:
time: 267 us
  waiting for transfers between devices  164 us (61%)
  local copies, waits for them, and re-layouts  37.6 us (14%)
  other arithmetic  19.2 us (7%)
  starting transfers between devices  17.7 us (7%)
  matrix products  14.8 us (6%)
  between operations  13.5 us (5%)
    all_to_all x1, waiting for transfers between devices, shards(): lax.all_to_all(ordered, 'pair', split_axis=1, concat_axis=0, tiled=True)  115 us
    reduce_scatter x1, waiting for transfers between devices, shards(): lax.psum_scatter(jnp.dot(owned, masked, preferred_element_type=jnp.float3...  32.1 us
    reshape x2, local copies, waits for them, and re-layouts, shards(): tiles_local = dressed.reshape(local_pairs, slab_rows * block_count, 128)  17.6 us
    all_to_all x1, waiting for transfers between devices, shards(): lax.all_to_all(jnp.stack([blocked] * lax.axis_size('pair')), 'pair', 0, 0)  17 us
    all_to_all x1, local copies, waits for them, and re-layouts, shards(): lax.all_to_all(ordered, 'pair', split_axis=1, concat_axis=0, tiled=True)  11.8 us
    all_to_all x1, starting transfers between devices, shards(): lax.all_to_all(jnp.stack([blocked] * lax.axis_size('pair')), 'pair', 0, 0)  11.7 us
    dot_general x1, matrix products, shards(): jnp.dot(flattened, gathered_cycle, preferred_element_type=jnp.float32)  10.5 us
    select_n x2, other arithmetic, shards(): jnp.take(tiles_local, slot_order, axis=1)  6.68 us
  transfers between devices with their start and end apart: 3, of which 3 were waited for; matrix products, arithmetic and copies ran while one was open for 5% of the time, Pallas kernels for 0%

profile of v1, /device:TPU:8, one launch (start us, length us, event | category | flops | bytes accessed | tf_op | source)
XLA Modules:
  0.0 266.6 jit_solution(9870551647190035924)
XLA Ops:
  6.5 0.9 select_reduce_fusion.3
  7.4 0.8 compare_select_fusion.2
  8.3 1.1 stack.2
  9.3 11.7 %all-to-all-start = ((bf16[32,20,640]{2,1,0:T(8,128)(2,1)}), bf16[32,20,640]{2,1,0:T(8,128)(2,1)S(1)}, u32[]{:S(2)}, u32[]{:S(2)}) async-start(bf16[32,20,640]{2,1,0:T(8,128)(2,1)} %stack.2), calls=%async_computation | async-start | bytes 1966080 | tf_op jit(solution)/shard_map/all_to_all | solution.py:39
  21.0 0.7 dynamic-slice_reduce_fusion
  21.9 0.7 fusion.13
  22.6 0.9 select_reduce_fusion.2
  23.5 0.8 broadcast_xor_fusion
  24.3 6.4 %compare_select_fusion = bf16[64,64,640]{2,1,0:T(8,128)(2,1)} fusion(bf16[64,64,640]{2,1,0:T(8,128)(2,1)} %param.7, s32[64,640]{1,0:T(8,128)S(1)} %broadcast_xor_fusion, s32[64]{0:T(128)} %param.11), kind=kLoop, calls=%fused_computation.2 | loop fusion | flops 5242880 | bytes 10649856 | tf_op jit(solution)/shard_map/jit(_where)/select_n | solution.py:32
  30.7 17.0 %all-to-all-done = bf16[32,20,640]{2,1,0:T(8,128)(2,1)S(1)} async-done(((bf16[32,20,640]{2,1,0:T(8,128)(2,1)}), bf16[32,20,640]{2,1,0:T(8,128)(2,1)S(1)}, u32[]{:S(2)}, u32[]{:S(2)}) %all-to-all-start) | async-done | bytes 819232 | tf_op jit(solution)/shard_map/all_to_all | solution.py:39
  47.8 10.5 %add_convert_fusion = bf16[4096,640]{1,0:T(8,128)(2,1)} fusion(bf16[4096,640]{1,0:T(8,128)(2,1)} %bitcast.44, bf16[640,640]{1,0:T(8,128)(2,1)S(1)} %reshape.271), kind=kOutput, calls=%fused_computation.1 | convolution fusion | flops 3363307520 | bytes 11304960 | tf_op jit(solution)/shard_map/dot_general | solution.py:41
  58.3 9.4 %reshape.272 = bf16[64,320,128]{2,1,0:T(8,128)(2,1)} reshape(bf16[4096,640]{1,0:T(8,128)(2,1)} %add_convert_fusion) | data formatting | bytes 10485760 | tf_op jit(solution)/shard_map/reshape | solution.py:43
  67.7 8.2 %copy.10 = bf16[64,320,128]{2,0,1:T(8,128)(2,1)} copy(bf16[64,320,128]{2,1,0:T(8,128)(2,1)} %reshape.272) | data formatting | bytes 10485760 | tf_op jit(solution)/shard_map/reshape | solution.py:43
  75.9 6.1 %gather_fusion = bf16[320,64,128]{2,1,0:T(8,128)(2,1)} fusion(bf16[64,320,128]{2,0,1:T(8,128)(2,1)} %copy.10, s32[1024]{0:T(1024)S(1)} %pad_clamp_fusion), kind=kCustom, calls=%fused_computation | custom fusion | bytes 10487040 | tf_op jit(solution)/shard_map/jit(_take)/gather | solution.py:46
  82.1 5.9 %broadcast_select_fusion = bf16[64,32,10,128]{3,0,2,1:T(8,128)(2,1)} fusion(bf16[64,32,10,128]{3,0,2,1:T(8,128)(2,1)} %bitcast.42, pred[32,10]{1,0:T(8,128)(4,1)S(1)} %compare_and_fusion), kind=kLoop, calls=%fused_computation.6 | loop fusion | flops 2621440 | bytes 10486080 | tf_op jit(solution)/shard_map/jit(_take)/select_n | solution.py:46
  88.0 5.7 %all-to-all-start.1 = ((bf16[64,32,10,128]{3,0,2,1:T(8,128)(2,1)}), bf16[64,32,10,128]{3,0,2,1:T(8,128)(2,1)}, u32[]{:S(2)}, u32[]{:S(2)}) async-start(bf16[64,32,10,128]{3,0,2,1:T(8,128)(2,1)} %broadcast_select_fusion), calls=%async_computation.1 | async-start | bytes 10485760 | tf_op jit(solution)/shard_map/all_to_all | solution.py:65
  93.8 0.2 reduce-scatter.2.cloned.1.call-start
  94.4 0.8 fusion.16
  95.7 0.3 select_reduce_fusion.1
  96.0 0.6 select_reduce_fusion
  96.8 114.6 %all-to-all-done.1 = bf16[64,32,10,128]{3,0,2,1:T(8,128)(2,1)} async-done(((bf16[64,32,10,128]{3,0,2,1:T(8,128)(2,1)}), bf16[64,32,10,128]{3,0,2,1:T(8,128)(2,1)}, u32[]{:S(2)}, u32[]{:S(2)}) %all-to-all-start.1) | async-done | bytes 5242912 | tf_op jit(solution)/shard_map/all_to_all | solution.py:65
  211.4 11.8 %copy.11 = bf16[32,64,1,10,128]{4,3,1,0,2:T(8,128)(2,1)S(1)} copy(bf16[32,64,1,10,128]{4,1,3,0,2:T(8,128)(2,1)} %bitcast.5) | data formatting | bytes 10485760 | tf_op jit(solution)/shard_map/all_to_all | solution.py:65
  223.2 4.4 %fusion.3 = bf16[2048,512]{1,0:T(8,128)(2,1)} fusion(bf16[256,8,10,128]{3,2,1,0:T(8,128)(2,1)S(1)} %bitcast.43, bf16[1,1,1280,512]{3,2,1,0:T(8,128)(2,1)S(1)} %copy-done.2, s32[512]{0:T(512)S(1)} %xor_bitcast_fusion.1, s32[1280]{0:T(1024)S(1)} %xor_bitcast_fusion), kind=kOutput, calls=%fused_computation.9 | convolution fusion | flops 2686713856 | bytes 8657920 | tf_op jit(solution)/shard_map/dot_general | solution.py:68
  227.6 32.1 %reduce-scatter.2.cloned.1.call-done = bf16[256,512]{1,0:T(8,128)(2,1)} async-done(((bf16[2048,512]{1,0:T(8,128)(2,1)}), bf16[256,512]{1,0:T(8,128)(2,1)}) %reduce-scatter.2.cloned.1.call-update) | async-done | bytes 262160 | tf_op jit(solution)/shard_map/reduce_scatter | solution.py:67
  (22 shorter events, 1.4 us)
Async XLA Ops:
  9.3 38.4 %all-to-all-start = ((bf16[32,20,640]{2,1,0:T(8,128)(2,1)}), bf16[32,20,640]{2,1,0:T(8,128)(2,1)S(1)}, u32[]{:S(2)}, u32[]{:S(2)}) async-start(bf16[32,20,640]{2,1,0:T(8,128)(2,1)} %stack.2), calls=%async_computation | async-start | bytes 1966080 | tf_op jit(solution)/shard_map/all_to_all | solution.py:39
  88.0 6.0 %copy-start.1 = (s32[32,4]{0,1:T(4,128)S(1)}, s32[32,4]{0,1:T(4,128)}, u32[]{:S(2)}) copy-start(s32[32,4]{0,1:T(4,128)} %param.13) | copy-start | bytes 1540
  88.0 7.2 %copy-start = (s32[640]{0:T(1024)S(1)}, s32[640]{0:T(1024)}, u32[]{:S(2)}) copy-start(s32[640]{0:T(1024)} %param.10) | copy-start | bytes 7684
  88.0 123.4 %all-to-all-start.1 = ((bf16[64,32,10,128]{3,0,2,1:T(8,128)(2,1)}), bf16[64,32,10,128]{3,0,2,1:T(8,128)(2,1)}, u32[]{:S(2)}, u32[]{:S(2)}) async-start(bf16[64,32,10,128]{3,0,2,1:T(8,128)(2,1)} %broadcast_select_fusion), calls=%async_computation.1 | async-start | bytes 10485760 | tf_op jit(solution)/shard_map/all_to_all | solution.py:65
  93.8 166.0 %reduce-scatter.2.cloned.1.call-start = ((), (), s32[]{:S(2)}) async-start(), calls=%async_computation.3 | async-start | bytes 2359296 | tf_op jit(solution)/shard_map/reduce_scatter | solution.py:67
  211.4 11.8 %copy-start.2 = (bf16[1,1,1280,512]{3,2,1,0:T(8,128)(2,1)S(1)}, bf16[1,1,1280,512]{3,2,1,0:T(8,128)(2,1)}, u32[]{:S(2)}) copy-start(bf16[1,1,1280,512]{3,2,1,0:T(8,128)(2,1)} %param.9) | copy-start | bytes 3932164
Sparse Core Ops, SparseCore 0:
  227.7 31.9 reduce-scatter.1
